TPU v7x, 256 devices: a whole 4x4x8 slice. The times are simulated.
256 devices in a mesh: req: 4 (over z_lo, core), exp: 64 (over y, x, z_hi).
Axes of the slice: x: 4, y: 4, z: 8 (z_hi: 4, z_lo: 2; z = z_hi * 2 + z_lo), core: 2. Of those that a mesh axis runs over, the one named last changes fastest.
Arguments:
- residual: bfloat16 [8192, 2048], P('exp'), may hold values from -6 to 6
- queries: bfloat16 [8192, 2048], P('exp', 'req'), may hold values from -128 to 128, as said below
- prefix_kv: bfloat16 [4, 16384, 256], P('req', 'exp'), may hold values from -4.5 to 4.5
- suffix_kv: bfloat16 [8192, 4, 256], P('exp', 'req'), may hold values from -6 to 6
- suffix_lengths: int32 [64, 4], P('exp'), may hold values from 1 to 96, 128 in all within a row
- out_proj: bfloat16 [2048, 2048], P('req'), may hold values from -0.5 to 0.5
- norm_gain: bfloat16 [2048], replicated, may hold values from 0.099609375 to 1.8984375
- routes: int32 [8192, 6], P('exp'), may hold values from 0 to 63, all different within a row; in each aligned block of 128 rows (0 to 127, 128 to 255, ...) at most 24 rows name the same one
- route_weights: float32 [8192, 6], P('exp'), may hold values from 0.1 to 0.5
- expert_gate: bfloat16 [64, 2048, 1408], P('exp', None, 'req'), may hold values from -0.125 to 0.125
- expert_up: bfloat16 [64, 2048, 1408], P('exp', None, 'req'), may hold values from -0.125 to 0.125
- expert_down: bfloat16 [64, 1408, 2048], P('exp', 'req'), may hold values from -0.15625 to 0.15625
- shared_gate: bfloat16 [2048, 1408], P(None, 'req'), may hold values from -0.125 to 0.125
- shared_up: bfloat16 [2048, 1408], P(None, 'req'), may hold values from -0.125 to 0.125
- shared_down: bfloat16 [1408, 2048], P('req'), may hold values from -0.15625 to 0.15625
Outputs:
- layer_out: bfloat16 [8192, 2048], P('exp')
Inputs may be any that keep to these rules, and one draw needn't show every extreme that they name: In the hidden draw some queries are strong multiples of prefix keys. `suffix_lengths`: each row (the requests of one index of exp) sums to 128, and in every row one request has exactly 96 tokens. `routes`: the 6 experts of a token are different. Among the 128 tokens of one index of exp no expert is picked more than 24 times, and in every draw some expert is picked exactly 24 times by the tokens of some index of exp.
All inputs are finite; a program needn't handle non-finite values.
Results may differ from a plain program's by a relative error of at most 0.015.
Values may be sent and summed in bfloat16 or wider, within the bound.
A program may use at most 128 MiB of HBM per device.

v0:
```python
import math

import jax
import jax.numpy as jnp
from jax import lax
from jax.sharding import PartitionSpec as P

HD = 128
TOP = 6


neg_big = -1e30
norm_eps = 1e-06


def on_device(
    residual,
    queries,
    prefix_kv,
    suffix_kv,
    suffix_lengths,
    out_proj,
    norm_gain,
    routes,
    route_weights,
    expert_gate,
    expert_up,
    expert_down,
    shared_gate,
    shared_up,
    shared_down,
):
    tokens_here = residual.shape[0]
    feat_width = residual.shape[1]
    head_count = queries.shape[1] // HD
    scaling = 1.0 / math.sqrt(HD)
    query_heads = jnp.transpose(queries.reshape(tokens_here, head_count, HD), (1, 0, 2))
    start_state = (
        jnp.full((head_count, tokens_here), neg_big, jnp.float32),
        jnp.zeros((head_count, tokens_here), jnp.float32),
        jnp.zeros((head_count, tokens_here, HD), jnp.float32),
    )

    def absorb(carried, key_rows, value_rows, allowed):
        running_max, running_sum, running_acc = carried
        scores = (
            jnp.einsum("htd,kd->htk", query_heads, key_rows, preferred_element_type=jnp.float32)
            * scaling
        )
        if allowed is not None:
            scores = jnp.where(allowed[None], scores, neg_big)
        new_max = jnp.maximum(running_max, jnp.max(scores, axis=-1))
        factor = jnp.exp(running_max - new_max)
        exp_scores = jnp.exp(scores - new_max[..., None])
        new_sum = running_sum * factor + jnp.sum(exp_scores, axis=-1)
        new_acc = running_acc * factor[..., None] + jnp.einsum(
            "htk,kd->htd",
            exp_scores.astype(jnp.bfloat16),
            value_rows,
            preferred_element_type=jnp.float32,
        )
        return (new_max, new_sum, new_acc)

    portion = lax.all_gather(prefix_kv, "exp", axis=1, tiled=True)
    key_count = portion.shape[1]
    window_len = math.gcd(key_count, 2048)

    def inner(position, inner_state):
        window = lax.dynamic_slice_in_dim(portion[0], position * window_len, window_len, 0)
        return absorb(inner_state, window[:, :HD], window[:, HD:], None)

    carried = lax.fori_loop(0, key_count // window_len, inner, start_state)
    request_ends = jnp.cumsum(suffix_lengths[0])
    positions = jnp.arange(tokens_here, dtype=jnp.int32)
    request_ids = jnp.sum((positions[:, None] >= request_ends[None, :]).astype(jnp.int32), axis=1)
    allowed = (request_ids[:, None] == request_ids[None, :]) & (
        positions[None, :] <= positions[:, None]
    )
    carried = absorb(carried, suffix_kv[:, 0, :HD], suffix_kv[:, 0, HD:], allowed)
    running_max, running_sum, running_acc = carried
    attention = (
        jnp.transpose(running_acc / running_sum[..., None], (1, 0, 2))
        .reshape(tokens_here, head_count * HD)
        .astype(jnp.bfloat16)
    )
    attn_terms = jnp.dot(attention, out_proj, preferred_element_type=jnp.float32)
    attn_out = lax.psum(attn_terms.astype(jnp.bfloat16), "req").astype(jnp.float32)
    hidden_state = (residual.astype(jnp.float32) + attn_out).astype(jnp.bfloat16)
    hidden_float = hidden_state.astype(jnp.float32)
    mean_square = jnp.mean(hidden_float * hidden_float, axis=-1, keepdims=True)
    normed = (
        hidden_float * lax.rsqrt(mean_square + norm_eps) * norm_gain.astype(jnp.float32)
    ).astype(jnp.bfloat16)
    shared_gate_act = jnp.dot(normed, shared_gate, preferred_element_type=jnp.float32)
    shared_up_act = jnp.dot(normed, shared_up, preferred_element_type=jnp.float32)
    shared_hidden = (jax.nn.silu(shared_gate_act) * shared_up_act).astype(jnp.bfloat16)
    shared_part = jnp.dot(shared_hidden, shared_down, preferred_element_type=jnp.float32)
    exp_count = lax.axis_size("exp")
    experts = exp_count * expert_gate.shape[0]
    capacity = min(tokens_here, 4 * ((tokens_here * TOP + 2 * experts - 1) // (2 * experts)))
    pick_ids = routes.reshape(-1)
    one_hot = (pick_ids[:, None] == jnp.arange(experts, dtype=jnp.int32)[None, :]).astype(jnp.int32)
    pick_ranks = jnp.sum((jnp.cumsum(one_hot, axis=0) - one_hot) * one_hot, axis=1)
    pick_slots = (pick_ids * capacity + pick_ranks).reshape(tokens_here, TOP)
    slot_ids = jnp.arange(experts * capacity, dtype=jnp.int32)
    placement = jnp.any(pick_slots[None, :, :] == slot_ids[:, None, None], axis=2).astype(
        jnp.bfloat16
    )
    buffer = (
        jnp.dot(placement, normed, preferred_element_type=jnp.float32)
        .astype(jnp.bfloat16)
        .reshape(experts, capacity, feat_width)
    )
    source_rows = lax.all_to_all(buffer, "exp", split_axis=0, concat_axis=0, tiled=True)
    sources, slot_count, row_width = source_rows.shape
    flat_rows = source_rows.reshape(sources * slot_count, row_width)
    gate_act = jnp.dot(flat_rows, expert_gate[0], preferred_element_type=jnp.float32)
    up_act = jnp.dot(flat_rows, expert_up[0], preferred_element_type=jnp.float32)
    expert_hidden = (jax.nn.silu(gate_act) * up_act).astype(jnp.bfloat16)
    partial_out = jnp.dot(expert_hidden, expert_down[0], preferred_element_type=jnp.float32).astype(
        jnp.bfloat16
    )
    finish_partial_out = partial_out.reshape(sources, slot_count, row_width)
    returned = lax.all_to_all(finish_partial_out, "exp", split_axis=0, concat_axis=0, tiled=True)
    flat_back = returned.reshape(experts * capacity, feat_width)
    picked_rows = (
        flat_back[pick_slots.reshape(-1)].astype(jnp.float32).reshape(tokens_here, TOP, feat_width)
    )
    routed = jnp.sum(picked_rows * route_weights[:, :, None], axis=1)
    summed = lax.psum((shared_part + routed).astype(jnp.bfloat16), "req").astype(jnp.float32)
    return (hidden_float + summed).astype(jnp.bfloat16)


def solution(mesh):
    placed = (
        P("exp", None),
        P("exp", "req"),
        P("req", "exp", None),
        P("exp", "req", None),
        P("exp", None),
        P("req", None),
        P(),
        P("exp", None),
        P("exp", None),
        P("exp", None, "req"),
        P("exp", None, "req"),
        P("exp", "req", None),
        P(None, "req"),
        P(None, "req"),
        P("req", None),
    )
    return jax.shard_map(
        on_device, mesh=mesh, in_specs=placed, out_specs=P("exp", None), check_vma=False
    )
```

profile of v0, /device:TPU:1, one launch (start us, length us, event | category | flops | bytes accessed | tf_op | source)
XLA Modules:
  0.0 634.4 jit_solution(8159375901670634559)
XLA Ops:
  16.8 104.8 %all-gather.2.cloned.1.call-done = bf16[1,16384,256]{2,1,0:T(8,128)(2,1)} async-done(((bf16[1,256,256]{2,1,0:T(8,128)(2,1)}), bf16[1,16384,256]{2,1,0:T(8,128)(2,1)}) %all-gather.2.cloned.1.call-update) | async-done | bytes 8388624 | tf_op jit(solution)/shard_map/all_gather | solution.py:64
  121.6 67.1 %while.18 = (s32[]{:T(128)}, f32[4,128]{1,0:T(4,128)S(1)}, f32[4,128]{1,0:T(4,128)S(1)}, f32[4,128,128]{2,1,0:T(8,128)S(1)}, bf16[1,16384,256]{2,1,0:T(8,128)(2,...) while((s32[]{:T(128)}, f32[4,128]{1,0:T(4,128)S(1)}, ...), condition=%wide.region_3.0_spmd.clone, body=%wide.region_0.0_spmd.clone.sunk | while | flops 545458688 | bytes 33194172 | solution.py:72
  125.6 3.0 fusion.75
  131.3 2.7 bitcast_reduce_fusion.2
  134.0 3.0 fusion.75
  139.7 2.7 bitcast_reduce_fusion.2
  142.4 3.0 fusion.75
  150.8 3.0 fusion.75
  156.5 2.7 bitcast_reduce_fusion.2
  159.2 3.0 fusion.75
  167.6 3.0 fusion.75
  175.9 3.0 fusion.75
  184.3 3.0 fusion.75
  194.4 48.7 %all-reduce.3.cloned.1.call-done = bf16[128,2048]{1,0:T(8,128)(2,1)} async-done(((bf16[128,2048]{1,0:T(8,128)(2,1)}), bf16[128,2048]{1,0:T(8,128)(2,1)}) %all-reduce.3.cloned.1.call-update) | async-done | bytes 524304 | tf_op jit(solution)/shard_map/psum | solution.py:87
  247.5 126.4 %all_to_all.10 = bf16[64,24,2048]{2,1,0:T(8,128)(2,1)S(1)} all-to-all(bf16[64,24,2048]{2,1,0:T(8,128)(2,1)S(1)} %bitcast.103), channel_id=1, replica_groups=mesh['req'=4,'exp'=64] {'exp'}, dimensions={0} | all-to-all | bytes 12582912 | tf_op jit(solution)/shard_map/all_to_all | solution.py:114
  376.6 3.8 fusion.18
  380.4 12.3 %convolution_convert_fusion = bf16[1536,2048]{1,0:T(8,128)(2,1)} fusion(bf16[1,352,2048]{2,1,0:T(8,128)(2,1)} %param.28, bf16[1536,2048]{1,0:T(8,128)(2,1)} %bitcast.106, f32[1536,352]{0,1:T(8,128)} %fusion.18, bf16[1,2048,352]{1,2,0:T(8,128)(2,1)} %param.27), kind=kOutput, calls=%fused_computation.21 | convolution fusion | flops 4435574784 | bytes 17629184 | tf_op jit(solution)/shard_map/dot_general | solution.py:120
  392.7 8.7 %all-to-all-start.1 = ((bf16[64,24,2048]{2,1,0:T(8,128)(2,1)}), bf16[64,24,2048]{2,1,0:T(8,128)(2,1)}, u32[]{:S(2)}, u32[]{:S(2)}) async-start(bf16[64,24,2048]{2,1,0:T(8,128)(2,1)} %bitcast.104), calls=%async_computation.1 | async-start | bytes 12582912 | tf_op jit(solution)/shard_map/all_to_all | solution.py:124
  402.5 139.7 %all-to-all-done.1 = bf16[64,24,2048]{2,1,0:T(8,128)(2,1)} async-done(((bf16[64,24,2048]{2,1,0:T(8,128)(2,1)}), bf16[64,24,2048]{2,1,0:T(8,128)(2,1)}, u32[]{:S(2)}, u32[]{:S(2)}) %all-to-all-start.1) | async-done | bytes 6291488 | tf_op jit(solution)/shard_map/all_to_all | solution.py:124
  542.2 10.7 %gather_fusion = bf16[768,2048]{1,0:T(8,128)(2,1)} fusion(bf16[1536,2048]{1,0:T(8,128)(2,1)} %bitcast.18, s32[1024]{0:T(1024)S(1)} %pad_clamp_fusion), kind=kCustom, calls=%fused_computation | custom fusion | bytes 6294528 | tf_op jit(solution)/shard_map/gather | solution.py:127
  552.9 6.6 %reshape.163 = f32[128,6,2048]{2,1,0:T(8,128)} reshape(bf16[768,2048]{1,0:T(8,128)(2,1)} %gather_fusion) | data formatting | bytes 9437184 | tf_op jit(solution)/shard_map/convert_element_type | solution.py:127
  559.5 7.6 %multiply_reduce_fusion = f32[128,2048]{1,0:T(8,128)} fusion(f32[128,6,2048]{2,1,0:T(8,128)} %reshape.163, f32[128,6]{1,0:T(8,128)S(1)} %copy.46), kind=kLoop, calls=%fused_computation.20 | loop fusion | flops 2883584 | bytes 7343104 | tf_op jit(solution)/shard_map/reduce_sum | solution.py:129
  567.1 4.5 fusion.15
  571.6 54.0 %all-reduce.5.cloned.1.call-done = bf16[128,2048]{1,0:T(8,128)(2,1)} async-done(((bf16[128,2048]{1,0:T(8,128)(2,1)}), bf16[128,2048]{1,0:T(8,128)(2,1)}) %all-reduce.5.cloned.1.call-update) | async-done | bytes 524304 | tf_op jit(solution)/shard_map/psum | solution.py:130
  (131 shorter events, 60.5 us)
Async XLA Ops:
  6.5 185.3 %copy-start = (bf16[512,2048]{1,0:T(8,128)(2,1)S(1)}, bf16[512,2048]{1,0:T(8,128)(2,1)}, u32[]{:S(2)}) copy-start(bf16[512,2048]{1,0:T(8,128)(2,1)} %param.22) | copy-start | bytes 6291460
  6.5 115.1 %all-gather.2.cloned.1.call-start = ((), (), s32[]{:S(2)}) async-start(), calls=%async_computation.2 | async-start | bytes 8519680 | tf_op jit(solution)/shard_map/all_gather | solution.py:64
  7.3 235.9 %all-reduce.3.cloned.1.call-start = ((), (), s32[]{:S(2)}) async-start(), calls=%async_computation.3 | async-start | bytes 1048576 | tf_op jit(solution)/shard_map/psum | solution.py:87
  8.1 3.6 copy-start.8
  13.5 108.1 %copy-start.5 = (s32[64,6,128]{2,0,1:T(8,128)}, s32[64,6,128]{2,0,1:T(8,128)S(1)}, u32[]{:S(2)}) copy-start(s32[64,6,128]{2,0,1:T(8,128)S(1)} %reduce-window.19) | copy-start | bytes 589828
  125.6 3.4 copy-start.2
  134.0 3.4 copy-start.2
  142.4 3.4 copy-start.2
  150.8 3.4 copy-start.2
  159.2 3.4 copy-start.2
  167.5 3.4 copy-start.2
  175.9 3.4 copy-start.2
  184.3 3.4 copy-start.2
  190.6 2.6 copy-start.6
  190.6 2.9 copy-start.9
  191.8 51.3 %copy-start.4 = (bf16[128,2048]{1,0:T(8,128)(2,1)S(1)}, bf16[128,2048]{1,0:T(8,128)(2,1)}, u32[]{:S(2)}) copy-start(bf16[128,2048]{1,0:T(8,128)(2,1)} %param.17) | copy-start | bytes 1572868
  191.8 52.6 %copy-start.10 = (f32[2048]{0:T(1024)S(1)}, f32[2048]{0:T(1024)}, u32[]{:S(2)}) copy-start(f32[2048]{0:T(1024)} %convert_element_type.89) | copy-start | bytes 24580
  247.5 129.1 %copy-start.13 = (bf16[1,2048,352]{1,2,0:T(8,128)(2,1)S(1)}, bf16[1,2048,352]{1,2,0:T(8,128)(2,1)}, u32[]{:S(2)}) copy-start(bf16[1,2048,352]{1,2,0:T(8,128)(2,1)} %param.26) | copy-start | bytes 4325380
  373.9 2.7 copy-start.3
  392.7 9.1 %copy-start.12 = (f32[128,6]{0,1:T(8,128)S(1)}, f32[128,6]{0,1:T(8,128)}, u32[]{:S(2)}) copy-start(f32[128,6]{0,1:T(8,128)} %param.25) | copy-start | bytes 9220
  392.7 9.3 %copy-start.7 = (bf16[2048,352]{0,1:T(8,128)(2,1)S(1)}, bf16[2048,352]{0,1:T(8,128)(2,1)}, u32[]{:S(2)}) copy-start(bf16[2048,352]{0,1:T(8,128)(2,1)} %param.29) | copy-start | bytes 4325380
  392.7 149.6 %all-to-all-start.1 = ((bf16[64,24,2048]{2,1,0:T(8,128)(2,1)}), bf16[64,24,2048]{2,1,0:T(8,128)(2,1)}, u32[]{:S(2)}, u32[]{:S(2)}) async-start(bf16[64,24,2048]{2,1,0:T(8,128)(2,1)} %bitcast.104), calls=%async_computation.1 | async-start | bytes 12582912 | tf_op jit(solution)/shard_map/all_to_all | solution.py:124
  401.4 224.3 %all-reduce.5.cloned.1.call-start = ((), (), s32[]{:S(2)}) async-start(), calls=%async_computation.4 | async-start | bytes 1048576 | tf_op jit(solution)/shard_map/psum | solution.py:130
  567.1 60.8 %copy-start.1 = (bf16[512,2048]{1,0:T(8,128)(2,1)S(1)}, bf16[512,2048]{1,0:T(8,128)(2,1)}, u32[]{:S(2)}) copy-start(bf16[512,2048]{1,0:T(8,128)(2,1)} %param.22) | copy-start | bytes 6291460
  (1 other events, 2.6 us)
Sparse Core Ops, SparseCore 0:
  10.6 110.9 all-gather.1
  193.3 49.7 all-reduce.2
  571.8 53.8 all-reduce.4
where the time goes:
time: 635 us; the launch traced here: 634 us
  waiting for transfers between devices  348 us (55%)
  blocking collectives  126 us (20%)
  matrix products  56.4 us (9%)
  other arithmetic  44.3 us (7%)
  local copies, waits for them, and re-layouts  36.5 us (6%)
  between operations  13.4 us (2%)
  starting transfers between devices  8.99 us (1%)
    all_to_all x1, waiting for transfers between devices, on_device(): lax.all_to_all(finish_partial_out, 'exp', split_axis=0, concat_axis=0, ti...  140 us
    all_to_all x1, blocking collectives, on_device(): lax.all_to_all(buffer, 'exp', split_axis=0, concat_axis=0, tiled=True)  126 us
    all_gather x1, waiting for transfers between devices, on_device(): portion = lax.all_gather(prefix_kv, 'exp', axis=1, tiled=True)  105 us
    psum x1, waiting for transfers between devices, on_device(): lax.psum((shared_part + routed).astype(jnp.bfloat16), 'req')  54 us
    psum x1, waiting for transfers between devices, on_device(): lax.psum(attn_terms.astype(jnp.bfloat16), 'req').astype(jnp.float32)  48.7 us
    reduce_sum x9, other arithmetic, absorb(): new_sum = running_sum * factor + jnp.sum(exp_scores, axis=-1)  25.3 us
    dot_general x9, matrix products, absorb(): jnp.einsum('htd,kd->htk', query_heads, key_rows, preferred_element_type=j...  23.7 us
  transfers between devices with their start and end apart: 4, of which 4 were waited for; matrix products, arithmetic and copies ran while one was open for 2% of the time, Pallas kernels for 0%

commit v1 on v0

v1 whole, which is shorter than its diff:
```python
import math

import jax
import jax.numpy as jnp
from jax import lax
from jax.experimental import pallas as pl
from jax.experimental.pallas import tpu as pltpu
from jax.sharding import PartitionSpec as P

HD = 128
TOP = 6
CAP = 24

neg_big = -1e30
norm_eps = 1e-06

CORE_SWAP = [(0, 1), (1, 0), (2, 3), (3, 2)]
CHIP_SWAP = [(0, 2), (2, 0), (1, 3), (3, 1)]

KEY_BLOCK = 2048
KEY_CHUNK = 512


def attend_kernel(q_ref, kv_ref, suffix_ref, mask_ref, out_ref, q_rows, top, total, acc):
    step = pl.program_id(0)
    tokens = q_ref.shape[0]
    heads = q_ref.shape[1] // HD
    scale = math.log2(math.e) / math.sqrt(HD)

    def score(keys):
        return lax.dot_general(
            keys, q_rows[...], (((1,), (1,)), ((), ())), preferred_element_type=jnp.float32
        ) * scale

    def weigh(values, weights):
        return lax.dot_general(
            values,
            weights.astype(jnp.bfloat16),
            (((0,), (0,)), ((), ())),
            preferred_element_type=jnp.float32,
        )

    @pl.when(step == 0)
    def _():
        for h in range(heads):
            q_rows[h * tokens : (h + 1) * tokens, :] = q_ref[:, h * HD : (h + 1) * HD]
        mask = jnp.concatenate([mask_ref[...]] * heads, axis=1)
        scores = jnp.where(mask > 0.5, score(suffix_ref[:, :HD]), neg_big)
        first = jnp.max(scores, axis=0, keepdims=True)
        weights = jnp.exp2(scores - first)
        top[...] = first
        total[...] = jnp.sum(weights, axis=0, keepdims=True)
        acc[...] = weigh(suffix_ref[:, HD:], weights)

    running_top, running_total, running_acc = top[...], total[...], acc[...]
    for c in range(KEY_BLOCK // KEY_CHUNK):
        rows = slice(c * KEY_CHUNK, (c + 1) * KEY_CHUNK)
        scores = score(kv_ref[0, rows, :HD])
        new_top = jnp.maximum(running_top, jnp.max(scores, axis=0, keepdims=True))
        factor = jnp.exp2(running_top - new_top)
        weights = jnp.exp2(scores - new_top)
        running_total = running_total * factor + jnp.sum(weights, axis=0, keepdims=True)
        running_acc = running_acc * factor + weigh(kv_ref[0, rows, HD:], weights)
        running_top = new_top
    top[...], total[...], acc[...] = running_top, running_total, running_acc

    @pl.when(step == pl.num_programs(0) - 1)
    def _():
        done = running_acc / running_total
        for h in range(heads):
            out_ref[:, h * HD : (h + 1) * HD] = done[:, h * tokens : (h + 1) * tokens].T.astype(
                jnp.bfloat16
            )


def attend(queries, prefix, suffix, mask):
    tokens, width = queries.shape
    columns = tokens * (width // HD)
    steps = prefix.shape[1] // KEY_BLOCK
    return pl.pallas_call(
        attend_kernel,
        grid=(steps,),
        out_shape=jax.ShapeDtypeStruct((tokens, width), jnp.bfloat16),
        in_specs=[
            pl.BlockSpec((tokens, width), lambda i: (0, 0)),
            pl.BlockSpec((1, KEY_BLOCK, 2 * HD), lambda i: (0, i, 0)),
            pl.BlockSpec(suffix.shape, lambda i: (0, 0)),
            pl.BlockSpec(mask.shape, lambda i: (0, 0)),
        ],
        out_specs=pl.BlockSpec((tokens, width), lambda i: (0, 0)),
        scratch_shapes=[
            pltpu.VMEM((columns, HD), jnp.bfloat16),
            pltpu.VMEM((1, columns), jnp.float32),
            pltpu.VMEM((1, columns), jnp.float32),
            pltpu.VMEM((HD, columns), jnp.float32),
        ],
        compiler_params=pltpu.CompilerParams(
            dimension_semantics=("arbitrary",), vmem_limit_bytes=40 * 1024 * 1024
        ),
        cost_estimate=pl.CostEstimate(
            flops=4 * columns * prefix.shape[1] * HD,
            bytes_accessed=prefix.size * 2,
            transcendentals=columns * prefix.shape[1],
        ),
        name="attend",
    )(queries, prefix, suffix, mask)


def half_sum(terms, core):
    half = terms.shape[0] // 2
    mine = lax.dynamic_slice_in_dim(terms, core * half, half, 0)
    other = lax.dynamic_slice_in_dim(terms, (1 - core) * half, half, 0)
    came = lax.ppermute(other, "req", CORE_SWAP)
    chip = lax.optimization_barrier(
        (mine.astype(jnp.float32) + came.astype(jnp.float32)).astype(jnp.bfloat16)
    )
    across = lax.ppermute(chip, "req", CHIP_SWAP)
    return chip.astype(jnp.float32) + across.astype(jnp.float32)


def whole_rows(half, core):
    half = lax.optimization_barrier(half)
    other = lax.ppermute(half, "req", CORE_SWAP)
    low = jnp.where(core == 0, half, other)
    high = jnp.where(core == 0, other, half)
    return jnp.concatenate([low, high], axis=0)


def on_device(
    residual,
    queries,
    prefix_kv,
    suffix_kv,
    suffix_lengths,
    out_proj,
    norm_gain,
    routes,
    route_weights,
    expert_gate,
    expert_up,
    expert_down,
    shared_gate,
    shared_up,
    shared_down,
):
    tokens_here, feat_width = residual.shape
    half = tokens_here // 2
    exp_count = lax.axis_size("exp")
    req_count = lax.axis_size("req")
    me = lax.axis_index("req")
    core = me % 2
    slots = CAP // req_count
    rows_here = exp_count * slots

    portion = lax.all_gather(prefix_kv, "exp", axis=1, tiled=True)

    own = (expert_gate[0], expert_up[0], expert_down[0])
    beside = tuple(lax.ppermute(w, "req", CORE_SWAP) for w in own)
    across = tuple(lax.ppermute(w, "req", CHIP_SWAP) for w in own)
    far = tuple(lax.ppermute(w, "req", CORE_SWAP) for w in across)

    request_ends = jnp.cumsum(suffix_lengths[0])
    positions = jnp.arange(tokens_here, dtype=jnp.int32)
    request_ids = jnp.sum((positions[:, None] >= request_ends[None, :]).astype(jnp.int32), axis=1)
    allowed = (request_ids[:, None] == request_ids[None, :]) & (
        positions[:, None] <= positions[None, :]
    )
    attention = attend(queries, portion, suffix_kv[:, 0, :], allowed.astype(jnp.float32))

    attn_terms = jnp.dot(attention, out_proj, preferred_element_type=jnp.float32)
    attn_half = half_sum(attn_terms.astype(jnp.bfloat16), core)
    residual_half = lax.dynamic_slice_in_dim(residual, core * half, half, 0)
    hidden_half = lax.optimization_barrier(
        (residual_half.astype(jnp.float32) + attn_half).astype(jnp.bfloat16)
    )
    hidden_float = hidden_half.astype(jnp.float32)
    mean_square = jnp.mean(hidden_float * hidden_float, axis=-1, keepdims=True)
    normed = whole_rows(
        (
            hidden_float * lax.rsqrt(mean_square + norm_eps) * norm_gain.astype(jnp.float32)
        ).astype(jnp.bfloat16),
        core,
    )

    pick_ids = routes.reshape(-1)
    experts = jnp.arange(exp_count, dtype=jnp.int32)
    one_hot = (pick_ids[:, None] == experts[None, :]).astype(jnp.int32)
    pick_ranks = jnp.sum((jnp.cumsum(one_hot, axis=0) - one_hot) * one_hot, axis=1)
    pick_slots = jnp.where(
        pick_ranks // slots == me, pick_ids * slots + pick_ranks % slots, -1
    ).reshape(tokens_here, TOP)
    slot_ids = jnp.arange(rows_here, dtype=jnp.int32)
    chosen = pick_slots[:, :, None] == slot_ids[None, None, :]
    placement = jnp.any(chosen, axis=1).astype(jnp.bfloat16)
    mix = jnp.sum(jnp.where(chosen, route_weights[:, :, None], 0.0), axis=1)
    mix_high = lax.reduce_precision(mix, 8, 7)
    mix_low = (mix - mix_high).astype(jnp.bfloat16)
    mix_high = mix_high.astype(jnp.bfloat16)

    lanes = feat_width // HD
    buffer = lax.dot_general(
        placement, normed, (((0,), (0,)), ((), ())), preferred_element_type=jnp.float32
    ).astype(jnp.bfloat16)
    sent = lax.all_to_all(
        buffer.reshape(exp_count, slots * lanes, HD), "exp", split_axis=0, concat_axis=0, tiled=True
    )
    source_rows = sent.reshape(rows_here, feat_width)

    shared_gate_act = jnp.dot(normed, shared_gate, preferred_element_type=jnp.float32)
    shared_up_act = jnp.dot(normed, shared_up, preferred_element_type=jnp.float32)
    shared_hidden = (jax.nn.silu(shared_gate_act) * shared_up_act).astype(jnp.bfloat16)
    shared_part = jnp.dot(shared_hidden, shared_down, preferred_element_type=jnp.float32)

    expert_out = jnp.zeros((rows_here, feat_width), jnp.float32)
    for gate, up, down in (own, beside, across, far):
        gate_act = jnp.dot(source_rows, gate, preferred_element_type=jnp.float32)
        up_act = jnp.dot(source_rows, up, preferred_element_type=jnp.float32)
        expert_hidden = (jax.nn.silu(gate_act) * up_act).astype(jnp.bfloat16)
        expert_out += jnp.dot(expert_hidden, down, preferred_element_type=jnp.float32)
    returned = lax.all_to_all(
        expert_out.astype(jnp.bfloat16).reshape(exp_count, slots * lanes, HD),
        "exp",
        split_axis=0,
        concat_axis=0,
        tiled=True,
    ).reshape(rows_here, feat_width)
    routed = jnp.dot(mix_high, returned, preferred_element_type=jnp.float32) + jnp.dot(
        mix_low, returned, preferred_element_type=jnp.float32
    )
    summed = half_sum((shared_part + routed).astype(jnp.bfloat16), core)
    return whole_rows((hidden_float + summed).astype(jnp.bfloat16), core)


def solution(mesh):
    placed = (
        P("exp", None),
        P("exp", "req"),
        P("req", "exp", None),
        P("exp", "req", None),
        P("exp", None),
        P("req", None),
        P(),
        P("exp", None),
        P("exp", None),
        P("exp", None, "req"),
        P("exp", None, "req"),
        P("exp", "req", None),
        P(None, "req"),
        P(None, "req"),
        P("req", None),
    )
    return jax.shard_map(
        on_device, mesh=mesh, in_specs=placed, out_specs=P("exp", None), check_vma=False
    )
```

time: 635 us -> 428 us (0.67)
  blocking collectives: 126 us -> 0 us
  waiting for transfers between devices: 348 us -> 265 us
  starting transfers between devices: 8.99 us -> 51.4 us
  other arithmetic: 44.3 us -> 6.71 us
  Pallas kernels: 0 us -> 18.6 us
  local copies, waits for them, and re-layouts: 36.5 us -> 22 us
  matrix products: 56.4 us -> 49.4 us
    all_to_all x1 -> x0, blocking collectives: 126 us -> none  [on_device(): lax.all_to_all(buffer, 'exp', split_axis=0, concat_axis=0, tiled=True)]
    ppermute x0 -> x15, waiting for transfers between devices: none -> 125 us  [the longest x3 109 us: on_device(): across = tuple((lax.ppermute(w, 'req', CHIP_SWAP) for w in own))]
    all_to_all x1 -> x2, waiting for transfers between devices: 140 us -> 29.3 us  [the longest x1 29.3 us: on_device(): lax.all_to_all(expert_out.astype(jnp.bfloat16).reshape(exp_count, slots *...]
    psum x2 -> x0, waiting for transfers between devices: 103 us -> none  [the longest x1 54 us: on_device(): lax.psum((shared_part + routed).astype(jnp.bfloat16), 'req')]
    reduce_sum x10 -> x1, other arithmetic: 32.9 us -> 0.95 us  [on_device(): mix = jnp.sum(jnp.where(chosen, route_weights[:, :, None], 0.0), axis=1)]
    ppermute x0 -> x15, starting transfers between devices: none -> 29.7 us  [the longest x2 12.8 us: half_sum(): came = lax.ppermute(other, 'req', CORE_SWAP)]
    pallas_call x0 -> x1, Pallas kernels: none -> 18.6 us  [attend(): pl.pallas_call(attend_kernel, grid=(steps,), out_shape=jax.ShapeDtypeStru...]
    reshape x0 -> x4, local copies, waits for them, and re-layouts: none -> 14.9 us  [the longest x1 3.75 us: on_device(): buffer.reshape(exp_count, slots * lanes, HD)]
  transfers between devices with their start and end apart: 4 -> 18, of which waited for: 4 -> 11; matrix products, arithmetic and copies ran while one was open for 2% -> 11% of each run, Pallas kernels for 0% -> 0%
where the time goes in v1:
time: 428 us; the launch traced here: 427 us
  waiting for transfers between devices  265 us (62%)
  starting transfers between devices  51.4 us (12%)
  matrix products  49.4 us (12%)
  local copies, waits for them, and re-layouts  22 us (5%)
  Pallas kernels  18.6 us (4%)
  between operations  13.7 us (3%)
  other arithmetic  6.71 us (2%)
    all_gather x1, waiting for transfers between devices, on_device(): portion = lax.all_gather(prefix_kv, 'exp', axis=1, tiled=True)  110 us
    ppermute x3, waiting for transfers between devices, on_device(): across = tuple((lax.ppermute(w, 'req', CHIP_SWAP) for w in own))  109 us
    all_to_all x1, waiting for transfers between devices, on_device(): lax.all_to_all(expert_out.astype(jnp.bfloat16).reshape(exp_count, slots *...  29.3 us
    dot_general x4, matrix products, on_device(): jnp.dot(expert_hidden, down, preferred_element_type=jnp.float32)  26.3 us
    pallas_call x1, Pallas kernels, attend(): pl.pallas_call(attend_kernel, grid=(steps,), out_shape=jax.ShapeDtypeStru...  18.6 us
    ppermute x2, starting transfers between devices, half_sum(): came = lax.ppermute(other, 'req', CORE_SWAP)  12.8 us
    ppermute x2, waiting for transfers between devices, half_sum(): across = lax.ppermute(chip, 'req', CHIP_SWAP)  12.3 us
    dot_general x4, matrix products, on_device(): gate_act = jnp.dot(source_rows, gate, preferred_element_type=jnp.float32)  12.2 us
  transfers between devices with their start and end apart: 18, of which 11 were waited for; matrix products, arithmetic and copies ran while one was open for 11% of the time, Pallas kernels for 0%

profile of v1, /device:TPU:1, one launch (start us, length us, event | category | flops | bytes accessed | tf_op | source)
XLA Modules:
  0.0 427.3 jit_solution(548454573659122724)
XLA Ops:
  11.5 110.1 %all-gather.2.cloned.1.call-done.kv_ref = bf16[1,16384,256]{2,1,0:T(8,128)(2,1)} async-done(((bf16[1,256,256]{2,1,0:T(8,128)(2,1)}), bf16[1,16384,256]{2,1,0:T(8,128)(2,1)}) %all-gather.2.cloned.1.call-update) | async-done | bytes 8388624 | tf_op jit(solution)/shard_map/all_gather | solution.py:155
  121.6 3.4 copy-done.1
  126.8 18.6 %attend.1 = bf16[128,512]{1,0:T(8,128)(2,1)S(1)} custom-call(bf16[128,512]{1,0:T(8,128)(2,1)S(1)} %copy-done.2, bf16[1,16384,256]{2,1,0:T(8,128)(2,1)S(1)} %copy-done.1, bf16[128,256]{1,0:T(8,128)(2,1)S(1)} %bitcast.58, f32[128,128]{1,0:T(8,128)S(1)} %fusion.35.mask_ref), custom_call_target="tpu_custom_call" | custom-call | flops 4294967296 | bytes 8388608 | tf_op jit(solution)/shard_map/attend/pallas_call | solution.py:80
  145.9 8.5 %collective-permute-start = (bf16[64,2048]{1,0:T(8,128)(2,1)S(1)}, bf16[64,2048]{1,0:T(8,128)(2,1)S(1)}, u32[]{:S(2)}, u32[]{:S(2)}) collective-permute-start(bf16[64,2048]{1,0:T(8,128)(2,1)S(1)} %constant_dynamic-slice_fusion.1), channel_id=1, source_target_pairs={{0,64},{64,0},{128,192},{192,128},{1,65},{65,1},{129,193},{193,129... | collective-permute-start | bytes 786440 | tf_op jit(solution)/shard_map/ppermute | solution.py:113
  157.1 6.0 %collective-permute-done.1 = bf16[64,2048]{1,0:T(8,128)(2,1)S(1)} collective-permute-done((bf16[64,2048]{1,0:T(8,128)(2,1)S(1)}, bf16[64,2048]{1,0:T(8,128)(2,1)S(1)}, u32[]{:S(2)}, u32[]{:S(2)}) %collective-permute-start.1) | collective-permute-done | bytes 262176 | tf_op jit(solution)/shard_map/ppermute | solution.py:117
  168.8 3.7 reshape.98
  172.6 9.8 %all-to-all-start = ((bf16[64,96,128]{2,1,0:T(8,128)(2,1)}), bf16[64,96,128]{2,1,0:T(8,128)(2,1)}, u32[]{:S(2)}, u32[]{:S(2)}) async-start(bf16[64,96,128]{2,1,0:T(8,128)(2,1)} %reshape.98), calls=%async_computation | async-start | bytes 3145728 | tf_op jit(solution)/shard_map/all_to_all | solution.py:204
  185.9 62.2 %collective-permute-done.6 = bf16[2048,352]{0,1:T(8,128)(2,1)} collective-permute-done((bf16[2048,352]{0,1:T(8,128)(2,1)}, bf16[2048,352]{0,1:T(8,128)(2,1)}, u32[]{:S(2)}, u32[]{:S(2)}) %collective-permute-start.6) | collective-permute-done | bytes 1441824 | tf_op jit(solution)/shard_map/ppermute | solution.py:159
  250.1 3.7 reshape.99
  253.8 3.7 fusion.43
  261.1 17.8 %collective-permute-done.7 = bf16[2048,352]{0,1:T(8,128)(2,1)} collective-permute-done((bf16[2048,352]{0,1:T(8,128)(2,1)}, bf16[2048,352]{0,1:T(8,128)(2,1)}, u32[]{:S(2)}, u32[]{:S(2)}) %collective-permute-start.7) | collective-permute-done | bytes 1441824 | tf_op jit(solution)/shard_map/ppermute | solution.py:159
  281.0 28.8 %collective-permute-done.8 = bf16[352,2048]{1,0:T(8,128)(2,1)} collective-permute-done((bf16[352,2048]{1,0:T(8,128)(2,1)}, bf16[352,2048]{1,0:T(8,128)(2,1)}, u32[]{:S(2)}, u32[]{:S(2)}) %collective-permute-start.8) | collective-permute-done | bytes 1441824 | tf_op jit(solution)/shard_map/ppermute | solution.py:159
  316.4 6.0 %fusion.4 = f32[384,2048]{1,0:T(8,128)} fusion(bf16[384,2048]{1,0:T(8,128)(2,1)} %reshape.99, f32[384,352]{0,1:T(8,128)} %fusion.43, bf16[1,352,2048]{2,1,0:T(8,128)(2,1)} %param.26, bf16[1,2048,352]{1,2,0:T(8,128)(2,1)} %param.25), kind=kOutput, calls=%fused_computation.11 | convolution fusion | flops 1108107264 | bytes 8142848 | tf_op jit(solution)/shard_map/dot_general | solution.py:219
  322.4 6.0 %fusion.15 = f32[384,2048]{1,0:T(8,128)} fusion(bf16[352,2048]{1,0:T(8,128)(2,1)} %collective-permute-done.8, f32[384,352]{0,1:T(8,128)} %fusion.57, bf16[384,2048]{1,0:T(8,128)(2,1)} %reshape.99, bf16[2048,352]{0,1:T(8,128)(2,1)} %collective-permute-done.7), kind=kOutput, calls=%fused_computation.35 | convolution fusion | flops 1108107264 | bytes 8142848 | tf_op jit(solution)/shard_map/dot_general | solution.py:219
  328.5 6.1 %fusion.14 = f32[384,2048]{1,0:T(8,128)} fusion(bf16[352,2048]{1,0:T(8,128)(2,1)} %collective-permute-done.5, f32[384,352]{0,1:T(8,128)} %fusion.56, bf16[384,2048]{1,0:T(8,128)(2,1)} %reshape.99, bf16[2048,352]{0,1:T(8,128)(2,1)} %collective-permute-done.4), kind=kOutput, calls=%fused_computation.34 | convolution fusion | flops 1108107264 | bytes 8142848 | tf_op jit(solution)/shard_map/dot_general | solution.py:219
  334.5 8.3 %add_convert_fusion = bf16[384,2048]{1,0:T(8,128)(2,1)} fusion(f32[384,2048]{1,0:T(8,128)} %fusion.15, f32[384,2048]{1,0:T(8,128)} %fusion.4, f32[384,2048]{1,0:T(8,128)} %fusion.14, bf16[352,2048]{1,0:T(8,128)(2,1)} %collective-permute-done.11, f32[384,352]{0,1:T(8,128)S(1)} %fusion.58, bf16[384,2048]{1,0:T(8,128)(2,1)} %reshape.99, ...), kind=kOutput, calls=%fused_computation | convolution fusion | flops 1111252992 | bytes 16007168 | tf_op jit(solution)/shard_map/dot_general | solution.py:219
  342.8 3.7 reshape.100
  346.5 11.9 %all-to-all-start.1 = ((bf16[64,96,128]{2,1,0:T(8,128)(2,1)}), bf16[64,96,128]{2,1,0:T(8,128)(2,1)}, u32[]{:S(2)}, u32[]{:S(2)}) async-start(bf16[64,96,128]{2,1,0:T(8,128)(2,1)} %reshape.100), calls=%async_computation.1 | async-start | bytes 3145728 | tf_op jit(solution)/shard_map/all_to_all | solution.py:220
  362.0 3.5 fusion.27
  365.5 29.3 %all-to-all-done.1 = bf16[64,96,128]{2,1,0:T(8,128)(2,1)} async-done(((bf16[64,96,128]{2,1,0:T(8,128)(2,1)}), bf16[64,96,128]{2,1,0:T(8,128)(2,1)}, u32[]{:S(2)}, u32[]{:S(2)}) %all-to-all-start.1) | async-done | bytes 1572896 | tf_op jit(solution)/shard_map/all_to_all | solution.py:220
  394.8 3.7 reshape.101
  401.1 4.3 %collective-permute-start.12 = (bf16[64,2048]{1,0:T(8,128)(2,1)S(1)}, bf16[64,2048]{1,0:T(8,128)(2,1)S(1)}, u32[]{:S(2)}, u32[]{:S(2)}) collective-permute-start(bf16[64,2048]{1,0:T(8,128)(2,1)S(1)} %constant_dynamic-slice_fusion), channel_id=1, source_target_pairs={{0,64},{64,0},{128,192},{192,128},{1,65},{65,1},{129,193},{193,129... | collective-permute-start | bytes 786440 | tf_op jit(solution)/shard_map/ppermute | solution.py:113
  406.7 4.2 collective-permute-start.13
  410.9 6.3 %collective-permute-done.13 = bf16[64,2048]{1,0:T(8,128)(2,1)S(1)} collective-permute-done((bf16[64,2048]{1,0:T(8,128)(2,1)S(1)}, bf16[64,2048]{1,0:T(8,128)(2,1)S(1)}, u32[]{:S(2)}, u32[]{:S(2)}) %collective-permute-start.13) | collective-permute-done | bytes 262176 | tf_op jit(solution)/shard_map/ppermute | solution.py:117
  (91 shorter events, 43.8 us)
Async XLA Ops:
  6.5 138.8 %copy-start = (bf16[512,2048]{1,0:T(8,128)(2,1)S(1)}, bf16[512,2048]{1,0:T(8,128)(2,1)}, u32[]{:S(2)}) copy-start(bf16[512,2048]{1,0:T(8,128)(2,1)} %param.20) | copy-start | bytes 6291460
  6.5 115.1 %all-gather.2.cloned.1.call-start = ((), (), s32[]{:S(2)}) async-start(), calls=%async_computation.2 | async-start | bytes 8519680 | tf_op jit(solution)/shard_map/all_gather | solution.py:155
  145.4 9.1 %copy-start.9 = (s32[128,6]{0,1:T(8,128)S(1)}, s32[128,6]{0,1:T(8,128)}, u32[]{:S(2)}) copy-start(s32[128,6]{0,1:T(8,128)} %param.22) | copy-start | bytes 9220
  145.8 10.7 %copy-start.10 = (bf16[2048]{0:T(1024)(128)(2,1)S(1)}, bf16[2048]{0:T(1024)(128)(2,1)}, u32[]{:S(2)}) copy-start(bf16[2048]{0:T(1024)(128)(2,1)} %param.21) | copy-start | bytes 12292
  145.9 9.6 %collective-permute-start = (bf16[64,2048]{1,0:T(8,128)(2,1)S(1)}, bf16[64,2048]{1,0:T(8,128)(2,1)S(1)}, u32[]{:S(2)}, u32[]{:S(2)}) collective-permute-start(bf16[64,2048]{1,0:T(8,128)(2,1)S(1)} %constant_dynamic-slice_fusion.1), channel_id=1, source_target_pairs={{0,64},{64,0},{128,192},{192,128},{1,65},{65,1},{129,193},{193,129... | collective-permute-start | bytes 786440 | tf_op jit(solution)/shard_map/ppermute | solution.py:113
  155.6 7.6 %collective-permute-start.1 = (bf16[64,2048]{1,0:T(8,128)(2,1)S(1)}, bf16[64,2048]{1,0:T(8,128)(2,1)S(1)}, u32[]{:S(2)}, u32[]{:S(2)}) collective-permute-start(bf16[64,2048]{1,0:T(8,128)(2,1)S(1)} %add_convert_fusion.3), channel_id=1, source_target_pairs={{0,128},{128,0},{64,192},{192,64},{1,129},{129,1},{65,193},{193,65... | collective-permute-start | bytes 786440 | tf_op jit(solution)/shard_map/ppermute | solution.py:117
  164.5 2.5 collective-permute-start.2
  167.0 192.4 %copy-start.6 = (bf16[64,2048]{1,0:T(8,128)(2,1)}, bf16[64,2048]{1,0:T(8,128)(2,1)S(1)}, u32[]{:S(2)}) copy-start(bf16[64,2048]{1,0:T(8,128)(2,1)S(1)} %get-tuple-element.7) | copy-start | bytes 786436
  167.1 192.4 %copy-start.7 = (bf16[64,2048]{1,0:T(8,128)(2,1)}, bf16[64,2048]{1,0:T(8,128)(2,1)S(1)}, u32[]{:S(2)}) copy-start(bf16[64,2048]{1,0:T(8,128)(2,1)S(1)} %get-tuple-element.8) | copy-start | bytes 786436
  172.6 77.5 %all-to-all-start = ((bf16[64,96,128]{2,1,0:T(8,128)(2,1)}), bf16[64,96,128]{2,1,0:T(8,128)(2,1)}, u32[]{:S(2)}, u32[]{:S(2)}) async-start(bf16[64,96,128]{2,1,0:T(8,128)(2,1)} %reshape.98), calls=%async_computation | async-start | bytes 3145728 | tf_op jit(solution)/shard_map/all_to_all | solution.py:204
  182.4 65.7 %collective-permute-start.6 = (bf16[2048,352]{0,1:T(8,128)(2,1)}, bf16[2048,352]{0,1:T(8,128)(2,1)}, u32[]{:S(2)}, u32[]{:S(2)}) collective-permute-start(bf16[2048,352]{0,1:T(8,128)(2,1)} %bitcast.60), channel_id=1, source_target_pairs={{0,128},{128,0},{64,192},{192,64},{1,129},{129,1},{65,193},{193,65... | collective-permute-start | bytes 4325384 | tf_op jit(solution)/shard_map/ppermute | solution.py:159
  183.5 77.2 %collective-permute-start.3 = (bf16[2048,352]{0,1:T(8,128)(2,1)}, bf16[2048,352]{0,1:T(8,128)(2,1)}, u32[]{:S(2)}, u32[]{:S(2)}) collective-permute-start(bf16[2048,352]{0,1:T(8,128)(2,1)} %bitcast.61), channel_id=1, source_target_pairs={{0,64},{64,0},{128,192},{192,128},{1,65},{65,1},{129,193},{193,129... | collective-permute-start | bytes 4325384 | tf_op jit(solution)/shard_map/ppermute | solution.py:158
  184.4 94.5 %collective-permute-start.7 = (bf16[2048,352]{0,1:T(8,128)(2,1)}, bf16[2048,352]{0,1:T(8,128)(2,1)}, u32[]{:S(2)}, u32[]{:S(2)}) collective-permute-start(bf16[2048,352]{0,1:T(8,128)(2,1)} %bitcast.62), channel_id=1, source_target_pairs={{0,128},{128,0},{64,192},{192,64},{1,129},{129,1},{65,193},{193,65... | collective-permute-start | bytes 4325384 | tf_op jit(solution)/shard_map/ppermute | solution.py:159
  184.8 125.0 %collective-permute-start.8 = (bf16[352,2048]{1,0:T(8,128)(2,1)}, bf16[352,2048]{1,0:T(8,128)(2,1)}, u32[]{:S(2)}, u32[]{:S(2)}) collective-permute-start(bf16[352,2048]{1,0:T(8,128)(2,1)} %bitcast.6), channel_id=1, source_target_pairs={{0,128},{128,0},{64,192},{192,64},{1,129},{129,1},{65,193},{193,65... | collective-permute-start | bytes 4325384 | tf_op jit(solution)/shard_map/ppermute | solution.py:159
  248.0 66.1 %collective-permute-start.9 = (bf16[2048,352]{0,1:T(8,128)(2,1)}, bf16[2048,352]{0,1:T(8,128)(2,1)}, u32[]{:S(2)}, u32[]{:S(2)}) collective-permute-start(bf16[2048,352]{0,1:T(8,128)(2,1)} %collective-permute-done.6), channel_id=1, source_target_pairs={{0,64},{64,0},{128,192},{192,128},{1,65},{65,1},{129,193},{193,129... | collective-permute-start | bytes 4325384 | tf_op jit(solution)/shard_map/ppermute | solution.py:160
  250.1 78.4 %collective-permute-start.4 = (bf16[2048,352]{0,1:T(8,128)(2,1)}, bf16[2048,352]{0,1:T(8,128)(2,1)}, u32[]{:S(2)}, u32[]{:S(2)}) collective-permute-start(bf16[2048,352]{0,1:T(8,128)(2,1)} %bitcast.63), channel_id=1, source_target_pairs={{0,64},{64,0},{128,192},{192,128},{1,65},{65,1},{129,193},{193,129... | collective-permute-start | bytes 4325384 | tf_op jit(solution)/shard_map/ppermute | solution.py:158
  260.6 67.8 %collective-permute-start.5 = (bf16[352,2048]{1,0:T(8,128)(2,1)}, bf16[352,2048]{1,0:T(8,128)(2,1)}, u32[]{:S(2)}, u32[]{:S(2)}) collective-permute-start(bf16[352,2048]{1,0:T(8,128)(2,1)} %bitcast.6), channel_id=1, source_target_pairs={{0,64},{64,0},{128,192},{192,128},{1,65},{65,1},{129,193},{193,129... | collective-permute-start | bytes 4325384 | tf_op jit(solution)/shard_map/ppermute | solution.py:158
  278.9 55.6 %collective-permute-start.10 = (bf16[2048,352]{0,1:T(8,128)(2,1)}, bf16[2048,352]{0,1:T(8,128)(2,1)}, u32[]{:S(2)}, u32[]{:S(2)}) collective-permute-start(bf16[2048,352]{0,1:T(8,128)(2,1)} %collective-permute-done.7), channel_id=1, source_target_pairs={{0,64},{64,0},{128,192},{192,128},{1,65},{65,1},{129,193},{193,129... | collective-permute-start | bytes 4325384 | tf_op jit(solution)/shard_map/ppermute | solution.py:160
  309.8 24.7 %collective-permute-start.11 = (bf16[352,2048]{1,0:T(8,128)(2,1)}, bf16[352,2048]{1,0:T(8,128)(2,1)}, u32[]{:S(2)}, u32[]{:S(2)}) collective-permute-start(bf16[352,2048]{1,0:T(8,128)(2,1)} %collective-permute-done.8), channel_id=1, source_target_pairs={{0,64},{64,0},{128,192},{192,128},{1,65},{65,1},{129,193},{193,129... | collective-permute-start | bytes 4325384 | tf_op jit(solution)/shard_map/ppermute | solution.py:160
  346.5 11.9 %copy-start.11 = (f32[128,6]{0,1:T(8,128)S(1)}, f32[128,6]{0,1:T(8,128)}, u32[]{:S(2)}) copy-start(f32[128,6]{0,1:T(8,128)} %param.23) | copy-start | bytes 9220
  346.5 48.3 %all-to-all-start.1 = ((bf16[64,96,128]{2,1,0:T(8,128)(2,1)}), bf16[64,96,128]{2,1,0:T(8,128)(2,1)}, u32[]{:S(2)}, u32[]{:S(2)}) async-start(bf16[64,96,128]{2,1,0:T(8,128)(2,1)} %reshape.100), calls=%async_computation.1 | async-start | bytes 3145728 | tf_op jit(solution)/shard_map/all_to_all | solution.py:220
  401.1 5.5 %collective-permute-start.12 = (bf16[64,2048]{1,0:T(8,128)(2,1)S(1)}, bf16[64,2048]{1,0:T(8,128)(2,1)S(1)}, u32[]{:S(2)}, u32[]{:S(2)}) collective-permute-start(bf16[64,2048]{1,0:T(8,128)(2,1)S(1)} %constant_dynamic-slice_fusion), channel_id=1, source_target_pairs={{0,64},{64,0},{128,192},{192,128},{1,65},{65,1},{129,193},{193,129... | collective-permute-start | bytes 786440 | tf_op jit(solution)/shard_map/ppermute | solution.py:113
  406.7 10.5 %collective-permute-start.13 = (bf16[64,2048]{1,0:T(8,128)(2,1)S(1)}, bf16[64,2048]{1,0:T(8,128)(2,1)S(1)}, u32[]{:S(2)}, u32[]{:S(2)}) collective-permute-start(bf16[64,2048]{1,0:T(8,128)(2,1)S(1)} %add_convert_fusion.1), channel_id=1, source_target_pairs={{0,128},{128,0},{64,192},{192,64},{1,129},{129,1},{65,193},{193,65... | collective-permute-start | bytes 786440 | tf_op jit(solution)/shard_map/ppermute | solution.py:117
  417.3 2.2 collective-permute-start.14
  (6 other events, 13.0 us)
Sparse Core Ops, SparseCore 0:
  10.6 110.9 all-gather.1

commit v2 on v1

--- a/solution.py
+++ b/solution.py
@@ -157,6 +157,7 @@
     own = (expert_gate[0], expert_up[0], expert_down[0])
     beside = tuple(lax.ppermute(w, "req", CORE_SWAP) for w in own)
     across = tuple(lax.ppermute(w, "req", CHIP_SWAP) for w in own)
+    portion, beside, across = lax.optimization_barrier((portion, beside, across))
     far = tuple(lax.ppermute(w, "req", CORE_SWAP) for w in across)
 
     request_ends = jnp.cumsum(suffix_lengths[0])
@@ -166,6 +167,7 @@
         positions[:, None] <= positions[None, :]
     )
     attention = attend(queries, portion, suffix_kv[:, 0, :], allowed.astype(jnp.float32))
+    attention, far = lax.optimization_barrier((attention, far))
 
     attn_terms = jnp.dot(attention, out_proj, preferred_element_type=jnp.float32)
     attn_half = half_sum(attn_terms.astype(jnp.bfloat16), core)

time: 428 us -> 386 us (0.902)
  waiting for transfers between devices: 265 us -> 195 us
  blocking collectives: 0 us -> 56.1 us
  starting transfers between devices: 51.4 us -> 24.4 us
    all_gather x1, waiting for transfers between devices: 110 us -> 0.01 us  [on_device(): portion = lax.all_gather(prefix_kv, 'exp', axis=1, tiled=True)]
    all_to_all x0 -> x1, blocking collectives: none -> 56.1 us  [on_device(): lax.all_to_all(buffer.reshape(exp_count, slots * lanes, HD), 'exp', split...]
    ppermute x3, waiting for transfers between devices: 109 us -> 144 us  [on_device(): across = tuple((lax.ppermute(w, 'req', CHIP_SWAP) for w in own))]
    ppermute x2, starting transfers between devices: 12.8 us -> 0.97 us  [half_sum(): came = lax.ppermute(other, 'req', CORE_SWAP)]
    all_to_all x1 -> x0, starting transfers between devices: 9.76 us -> none  [on_device(): lax.all_to_all(buffer.reshape(exp_count, slots * lanes, HD), 'exp', split...]
    all_to_all x1, starting transfers between devices: 11.9 us -> 6.34 us  [on_device(): lax.all_to_all(expert_out.astype(jnp.bfloat16).reshape(exp_count, slots *...]
    ppermute x3, starting transfers between devices: 1.45 us -> 6.17 us  [on_device(): beside = tuple((lax.ppermute(w, 'req', CORE_SWAP) for w in own))]
  transfers between devices with their start and end apart: 18 -> 17, of which waited for: 11 -> 10; matrix products, arithmetic and copies ran while one was open for 11% -> 3% of each run, Pallas kernels for 0% -> 5%
where the time goes in v2:
time: 386 us; the launch traced here: 385 us
  waiting for transfers between devices  195 us (51%)
  blocking collectives  56.1 us (15%)
  matrix products  48 us (12%)
  starting transfers between devices  24.4 us (6%)
  local copies, waits for them, and re-layouts  22 us (6%)
  Pallas kernels  18.5 us (5%)
  between operations  13.7 us (4%)
  other arithmetic  6.71 us (2%)
    ppermute x3, waiting for transfers between devices, on_device(): across = tuple((lax.ppermute(w, 'req', CHIP_SWAP) for w in own))  144 us
    all_to_all x1, blocking collectives, on_device(): lax.all_to_all(buffer.reshape(exp_count, slots * lanes, HD), 'exp', split...  56.1 us
    all_to_all x1, waiting for transfers between devices, on_device(): lax.all_to_all(expert_out.astype(jnp.bfloat16).reshape(exp_count, slots *...  33.1 us
    dot_general x4, matrix products, on_device(): jnp.dot(expert_hidden, down, preferred_element_type=jnp.float32)  26.3 us
    pallas_call x1, Pallas kernels, attend(): pl.pallas_call(attend_kernel, grid=(steps,), out_shape=jax.ShapeDtypeStru...  18.5 us
    ppermute x2, waiting for transfers between devices, half_sum(): across = lax.ppermute(chip, 'req', CHIP_SWAP)  13.1 us
    dot_general x4, matrix products, on_device(): gate_act = jnp.dot(source_rows, gate, preferred_element_type=jnp.float32)  10.9 us
  transfers between devices with their start and end apart: 17, of which 10 were waited for; matrix products, arithmetic and copies ran while one was open for 3% of the time, Pallas kernels for 5%

profile of v2, /device:TPU:1, one launch (start us, length us, event | category | flops | bytes accessed | tf_op | source)
XLA Modules:
  0.0 384.9 jit_solution(17753608753311906922)
XLA Ops:
  7.3 2.5 collective-permute-start.3
  12.6 30.6 %collective-permute-done.3 = bf16[2048,352]{0,1:T(8,128)(2,1)} collective-permute-done((bf16[2048,352]{0,1:T(8,128)(2,1)}, bf16[2048,352]{0,1:T(8,128)(2,1)}, u32[]{:S(2)}, u32[]{:S(2)}) %collective-permute-start.3) | collective-permute-done | bytes 1441824 | tf_op jit(solution)/shard_map/ppermute | solution.py:159
  43.2 4.9 %collective-permute-start.2 = (bf16[352,2048]{1,0:T(8,128)(2,1)}, bf16[352,2048]{1,0:T(8,128)(2,1)}, u32[]{:S(2)}, u32[]{:S(2)}) collective-permute-start(bf16[352,2048]{1,0:T(8,128)(2,1)} %bitcast.63), channel_id=1, source_target_pairs={{0,64},{64,0},{128,192},{192,128},{1,65},{65,1},{129,193},{193,129... | collective-permute-start | bytes 4325384 | tf_op jit(solution)/shard_map/ppermute | solution.py:158
  48.1 49.5 %collective-permute-done.4 = bf16[2048,352]{0,1:T(8,128)(2,1)} collective-permute-done((bf16[2048,352]{0,1:T(8,128)(2,1)}, bf16[2048,352]{0,1:T(8,128)(2,1)}, u32[]{:S(2)}, u32[]{:S(2)}) %collective-permute-start.4) | collective-permute-done | bytes 1441824 | tf_op jit(solution)/shard_map/ppermute | solution.py:159
  97.6 63.9 %collective-permute-done.5 = bf16[352,2048]{1,0:T(8,128)(2,1)} collective-permute-done((bf16[352,2048]{1,0:T(8,128)(2,1)}, bf16[352,2048]{1,0:T(8,128)(2,1)}, u32[]{:S(2)}, u32[]{:S(2)}) %collective-permute-start.5) | collective-permute-done | bytes 1441824 | tf_op jit(solution)/shard_map/ppermute | solution.py:159
  168.6 3.4 copy-done.1
  173.7 18.5 %attend.1 = bf16[128,512]{1,0:T(8,128)(2,1)S(1)} custom-call(bf16[128,512]{1,0:T(8,128)(2,1)S(1)} %copy-done.2, bf16[1,16384,256]{2,1,0:T(8,128)(2,1)S(1)} %copy-done.1, bf16[128,256]{1,0:T(8,128)(2,1)S(1)} %bitcast.58, f32[128,128]{1,0:T(8,128)S(1)} %fusion.36.mask_ref), custom_call_target="tpu_custom_call" | custom-call | flops 4294967296 | bytes 8388608 | tf_op jit(solution)/shard_map/attend/pallas_call | solution.py:80
  196.6 5.7 %collective-permute-done.10 = bf16[64,2048]{1,0:T(8,128)(2,1)S(1)} collective-permute-done((bf16[64,2048]{1,0:T(8,128)(2,1)S(1)}, bf16[64,2048]{1,0:T(8,128)(2,1)S(1)}, u32[]{:S(2)}, u32[]{:S(2)}) %collective-permute-start.10) | collective-permute-done | bytes 262176 | tf_op jit(solution)/shard_map/ppermute | solution.py:117
  207.8 3.7 reshape.98
  211.5 56.1 %all_to_all.10 = bf16[64,96,128]{2,1,0:T(8,128)(2,1)} all-to-all(bf16[64,96,128]{2,1,0:T(8,128)(2,1)} %reshape.98), channel_id=1, replica_groups=mesh['req'=4,'exp'=64] {'exp'}, dimensions={0} | all-to-all | bytes 3145728 | tf_op jit(solution)/shard_map/all_to_all | solution.py:206
  267.6 3.7 reshape.99
  271.3 3.7 fusion.58
  279.1 3.1 fusion.57
  282.2 6.0 %fusion.15 = f32[384,2048]{1,0:T(8,128)} fusion(bf16[352,2048]{1,0:T(8,128)(2,1)} %collective-permute-done.5, f32[384,352]{0,1:T(8,128)} %fusion.58, bf16[384,2048]{1,0:T(8,128)(2,1)} %reshape.99, bf16[2048,352]{0,1:T(8,128)(2,1)} %collective-permute-done.4), kind=kOutput, calls=%fused_computation.35 | convolution fusion | flops 1108107264 | bytes 8142848 | tf_op jit(solution)/shard_map/dot_general | solution.py:221
  288.2 6.0 %fusion.4 = f32[384,2048]{1,0:T(8,128)} fusion(bf16[384,2048]{1,0:T(8,128)(2,1)} %reshape.99, f32[384,352]{0,1:T(8,128)} %fusion.44, bf16[1,352,2048]{2,1,0:T(8,128)(2,1)} %param.26, bf16[1,2048,352]{1,2,0:T(8,128)(2,1)} %param.25), kind=kOutput, calls=%fused_computation.11 | convolution fusion | flops 1108107264 | bytes 8142848 | tf_op jit(solution)/shard_map/dot_general | solution.py:221
  294.2 6.0 %fusion.14 = f32[384,2048]{1,0:T(8,128)} fusion(bf16[352,2048]{1,0:T(8,128)(2,1)} %collective-permute-done.2, f32[384,352]{0,1:T(8,128)} %fusion.57, bf16[384,2048]{1,0:T(8,128)(2,1)} %reshape.99, bf16[2048,352]{0,1:T(8,128)(2,1)} %collective-permute-done.1), kind=kOutput, calls=%fused_computation.34 | convolution fusion | flops 1108107264 | bytes 8142848 | tf_op jit(solution)/shard_map/dot_general | solution.py:221
  300.2 8.2 %add_convert_fusion = bf16[384,2048]{1,0:T(8,128)(2,1)} fusion(f32[384,2048]{1,0:T(8,128)} %fusion.15, f32[384,2048]{1,0:T(8,128)} %fusion.4, f32[384,2048]{1,0:T(8,128)} %fusion.14, bf16[352,2048]{1,0:T(8,128)(2,1)} %collective-permute-done.8, f32[384,352]{0,1:T(8,128)S(1)} %fusion.59, bf16[384,2048]{1,0:T(8,128)(2,1)} %reshape.99, ...), kind=kOutput, calls=%fused_computation | convolution fusion | flops 1111252992 | bytes 16007168 | tf_op jit(solution)/shard_map/dot_general | solution.py:221
  308.5 3.7 reshape.100
  312.2 6.3 %all-to-all-start.1 = ((bf16[64,96,128]{2,1,0:T(8,128)(2,1)}), bf16[64,96,128]{2,1,0:T(8,128)(2,1)}, u32[]{:S(2)}, u32[]{:S(2)}) async-start(bf16[64,96,128]{2,1,0:T(8,128)(2,1)} %reshape.100), calls=%async_computation.1 | async-start | bytes 3145728 | tf_op jit(solution)/shard_map/all_to_all | solution.py:222
  319.6 2.6 fusion.27
  322.1 3.5 fusion.28
  325.7 33.1 %all-to-all-done.1 = bf16[64,96,128]{2,1,0:T(8,128)(2,1)} async-done(((bf16[64,96,128]{2,1,0:T(8,128)(2,1)}), bf16[64,96,128]{2,1,0:T(8,128)(2,1)}, u32[]{:S(2)}, u32[]{:S(2)}) %all-to-all-start.1) | async-done | bytes 1572896 | tf_op jit(solution)/shard_map/all_to_all | solution.py:222
  358.8 3.7 reshape.101
  367.1 7.5 %collective-permute-done.13 = bf16[64,2048]{1,0:T(8,128)(2,1)S(1)} collective-permute-done((bf16[64,2048]{1,0:T(8,128)(2,1)S(1)}, bf16[64,2048]{1,0:T(8,128)(2,1)S(1)}, u32[]{:S(2)}, u32[]{:S(2)}) %collective-permute-start.13) | collective-permute-done | bytes 262176 | tf_op jit(solution)/shard_map/ppermute | solution.py:117
  (92 shorter events, 34.9 us)
Async XLA Ops:
  6.5 185.7 %copy-start = (bf16[512,2048]{1,0:T(8,128)(2,1)S(1)}, bf16[512,2048]{1,0:T(8,128)(2,1)}, u32[]{:S(2)}) copy-start(bf16[512,2048]{1,0:T(8,128)(2,1)} %param.20) | copy-start | bytes 6291460
  6.5 155.0 %all-gather.2.cloned.1.call-start = ((), (), s32[]{:S(2)}) async-start(), calls=%async_computation.2 | async-start | bytes 8519680 | tf_op jit(solution)/shard_map/all_gather | solution.py:155
  7.3 35.9 %collective-permute-start.3 = (bf16[2048,352]{0,1:T(8,128)(2,1)}, bf16[2048,352]{0,1:T(8,128)(2,1)}, u32[]{:S(2)}, u32[]{:S(2)}) collective-permute-start(bf16[2048,352]{0,1:T(8,128)(2,1)} %bitcast.60), channel_id=1, source_target_pairs={{0,128},{128,0},{64,192},{192,64},{1,129},{129,1},{65,193},{193,65... | collective-permute-start | bytes 4325384 | tf_op jit(solution)/shard_map/ppermute | solution.py:159
  9.8 38.3 %collective-permute-start = (bf16[2048,352]{0,1:T(8,128)(2,1)}, bf16[2048,352]{0,1:T(8,128)(2,1)}, u32[]{:S(2)}, u32[]{:S(2)}) collective-permute-start(bf16[2048,352]{0,1:T(8,128)(2,1)} %bitcast.61), channel_id=1, source_target_pairs={{0,64},{64,0},{128,192},{192,128},{1,65},{65,1},{129,193},{193,129... | collective-permute-start | bytes 4325384 | tf_op jit(solution)/shard_map/ppermute | solution.py:158
  10.8 86.9 %collective-permute-start.4 = (bf16[2048,352]{0,1:T(8,128)(2,1)}, bf16[2048,352]{0,1:T(8,128)(2,1)}, u32[]{:S(2)}, u32[]{:S(2)}) collective-permute-start(bf16[2048,352]{0,1:T(8,128)(2,1)} %bitcast.64), channel_id=1, source_target_pairs={{0,128},{128,0},{64,192},{192,64},{1,129},{129,1},{65,193},{193,65... | collective-permute-start | bytes 4325384 | tf_op jit(solution)/shard_map/ppermute | solution.py:159
  12.3 85.3 %collective-permute-start.1 = (bf16[2048,352]{0,1:T(8,128)(2,1)}, bf16[2048,352]{0,1:T(8,128)(2,1)}, u32[]{:S(2)}, u32[]{:S(2)}) collective-permute-start(bf16[2048,352]{0,1:T(8,128)(2,1)} %bitcast.65), channel_id=1, source_target_pairs={{0,64},{64,0},{128,192},{192,128},{1,65},{65,1},{129,193},{193,129... | collective-permute-start | bytes 4325384 | tf_op jit(solution)/shard_map/ppermute | solution.py:158
  12.6 149.0 %collective-permute-start.5 = (bf16[352,2048]{1,0:T(8,128)(2,1)}, bf16[352,2048]{1,0:T(8,128)(2,1)}, u32[]{:S(2)}, u32[]{:S(2)}) collective-permute-start(bf16[352,2048]{1,0:T(8,128)(2,1)} %bitcast.62), channel_id=1, source_target_pairs={{0,128},{128,0},{64,192},{192,64},{1,129},{129,1},{65,193},{193,65... | collective-permute-start | bytes 4325384 | tf_op jit(solution)/shard_map/ppermute | solution.py:159
  43.2 118.4 %collective-permute-start.2 = (bf16[352,2048]{1,0:T(8,128)(2,1)}, bf16[352,2048]{1,0:T(8,128)(2,1)}, u32[]{:S(2)}, u32[]{:S(2)}) collective-permute-start(bf16[352,2048]{1,0:T(8,128)(2,1)} %bitcast.63), channel_id=1, source_target_pairs={{0,64},{64,0},{128,192},{192,128},{1,65},{65,1},{129,193},{193,129... | collective-permute-start | bytes 4325384 | tf_op jit(solution)/shard_map/ppermute | solution.py:158
  161.6 30.7 %collective-permute-start.6 = (bf16[2048,352]{0,1:T(8,128)(2,1)}, bf16[2048,352]{0,1:T(8,128)(2,1)}, u32[]{:S(2)}, u32[]{:S(2)}) collective-permute-start(bf16[2048,352]{0,1:T(8,128)(2,1)} %collective-permute-done.3), channel_id=1, source_target_pairs={{0,64},{64,0},{128,192},{192,128},{1,65},{65,1},{129,193},{193,129... | collective-permute-start | bytes 4325384 | tf_op jit(solution)/shard_map/ppermute | solution.py:161
  163.8 28.4 %collective-permute-start.7 = (bf16[2048,352]{0,1:T(8,128)(2,1)}, bf16[2048,352]{0,1:T(8,128)(2,1)}, u32[]{:S(2)}, u32[]{:S(2)}) collective-permute-start(bf16[2048,352]{0,1:T(8,128)(2,1)} %collective-permute-done.4), channel_id=1, source_target_pairs={{0,64},{64,0},{128,192},{192,128},{1,65},{65,1},{129,193},{193,129... | collective-permute-start | bytes 4325384 | tf_op jit(solution)/shard_map/ppermute | solution.py:161
  163.9 28.3 %collective-permute-start.8 = (bf16[352,2048]{1,0:T(8,128)(2,1)}, bf16[352,2048]{1,0:T(8,128)(2,1)}, u32[]{:S(2)}, u32[]{:S(2)}) collective-permute-start(bf16[352,2048]{1,0:T(8,128)(2,1)} %collective-permute-done.5), channel_id=1, source_target_pairs={{0,64},{64,0},{128,192},{192,128},{1,65},{65,1},{129,193},{193,129... | collective-permute-start | bytes 4325384 | tf_op jit(solution)/shard_map/ppermute | solution.py:161
  168.6 3.4 copy-start.1
  192.8 1.6 collective-permute-start.9
  194.5 7.8 %collective-permute-start.10 = (bf16[64,2048]{1,0:T(8,128)(2,1)S(1)}, bf16[64,2048]{1,0:T(8,128)(2,1)S(1)}, u32[]{:S(2)}, u32[]{:S(2)}) collective-permute-start(bf16[64,2048]{1,0:T(8,128)(2,1)S(1)} %add_convert_fusion.3), channel_id=1, source_target_pairs={{0,128},{128,0},{64,192},{192,64},{1,129},{129,1},{65,193},{193,65... | collective-permute-start | bytes 786440 | tf_op jit(solution)/shard_map/ppermute | solution.py:117
  203.6 2.3 collective-permute-start.11
  205.9 113.6 %copy-start.6 = (bf16[64,2048]{1,0:T(8,128)(2,1)}, bf16[64,2048]{1,0:T(8,128)(2,1)S(1)}, u32[]{:S(2)}) copy-start(bf16[64,2048]{1,0:T(8,128)(2,1)S(1)} %get-tuple-element.29) | copy-start | bytes 786436
  206.0 113.6 %copy-start.7 = (bf16[64,2048]{1,0:T(8,128)(2,1)}, bf16[64,2048]{1,0:T(8,128)(2,1)S(1)}, u32[]{:S(2)}) copy-start(bf16[64,2048]{1,0:T(8,128)(2,1)S(1)} %get-tuple-element.30) | copy-start | bytes 786436
  271.3 3.7 copy-start.5
  271.3 3.7 copy-start.12
  312.2 6.4 %copy-start.11 = (f32[128,6]{0,1:T(8,128)S(1)}, f32[128,6]{0,1:T(8,128)}, u32[]{:S(2)}) copy-start(f32[128,6]{0,1:T(8,128)} %param.23) | copy-start | bytes 9220
  312.2 46.6 %all-to-all-start.1 = ((bf16[64,96,128]{2,1,0:T(8,128)(2,1)}), bf16[64,96,128]{2,1,0:T(8,128)(2,1)}, u32[]{:S(2)}, u32[]{:S(2)}) async-start(bf16[64,96,128]{2,1,0:T(8,128)(2,1)} %reshape.100), calls=%async_computation.1 | async-start | bytes 3145728 | tf_op jit(solution)/shard_map/all_to_all | solution.py:222
  365.1 1.9 collective-permute-start.12
  367.0 7.6 %collective-permute-start.13 = (bf16[64,2048]{1,0:T(8,128)(2,1)S(1)}, bf16[64,2048]{1,0:T(8,128)(2,1)S(1)}, u32[]{:S(2)}, u32[]{:S(2)}) collective-permute-start(bf16[64,2048]{1,0:T(8,128)(2,1)S(1)} %add_convert_fusion.1), channel_id=1, source_target_pairs={{0,128},{128,0},{64,192},{192,64},{1,129},{129,1},{65,193},{193,65... | collective-permute-start | bytes 786440 | tf_op jit(solution)/shard_map/ppermute | solution.py:117
  374.7 2.5 collective-permute-start.14
  (6 other events, 10.1 us)
Sparse Core Ops, SparseCore 0:
  10.6 144.6 all-gather.1
